TPU v7x, 256 devices: a whole 4x4x8 slice. The times are simulated.
256 devices in a mesh: dp: 8 (over x, core), context: 32 (over z, y).
Axes of the slice: x: 4, y: 4, z: 8, core: 2. Of those that a mesh axis runs over, the one named last changes fastest.
Arguments:
- inputs: bfloat16 [8, 16384, 1024], P('dp', 'context'), may hold values from -6 to 6
- step_size: float32 [8, 16384], P('dp', 'context'), may hold values from 0.25 to 16387
- decay_rate: float32 [256], replicated, may hold values from 1.2207031e-05 to 0.125
- frequency: float32 [256], replicated, may hold values from -0.5 to 0.5
- input_proj: bfloat16 [1024, 512], replicated, may hold values from -0.1875 to 0.1875
- output_proj: bfloat16 [1024, 512], replicated, may hold values from -0.25 to 0.25
- skip_gain: float32 [1024], replicated, may hold values from 0.25 to 1.75
- cotangent: bfloat16 [8, 16384, 1024], P('dp', 'context'), may hold values from -6 to 6
Outputs:
- outputs: bfloat16 [8, 16384, 1024], P('dp', 'context')
- input_grad: bfloat16 [8, 16384, 1024], P('dp', 'context')
- input_proj_grad: float32 [1024, 512], P('context')
- output_proj_grad: float32 [1024, 512], P('context')
All inputs are finite; a program needn't handle non-finite values.
Results may differ from a plain program's by a relative error of at most 0.0036.
Values sent between devices are 32-bit elements; how exact they have to be, the bound alone decides.
A program may use at most 64 MiB of HBM per device.

v0:
```python
import jax
import jax.numpy as jnp
from jax import lax
from jax.sharding import PartitionSpec as P


def prefix(x, axis, combine, identity, reverse):
    peers, place = (lax.axis_size(axis), lax.axis_index(axis))
    everything = jax.tree.map(lambda part: lax.all_gather(part, axis), x)
    start = jax.tree.map(
        lambda part, zero: jnp.broadcast_to(jnp.asarray(zero, part.dtype), part.shape), x, identity
    )

    def lap(k, before):
        at = peers - 1 - k if reverse else k
        reached = at > place if reverse else at < place
        new = combine(before, jax.tree.map(lambda part: part[at], everything))
        return jax.tree.map(lambda a, b: jnp.where(reached, a, b), new, before)

    return lax.fori_loop(0, peers, lap, start)


def complex_combine(earlier_pair, later_pair):
    early_are, early_aim, early_bre, early_bim = earlier_pair
    later_are, later_aim, later_bre, later_bim = later_pair
    return (
        later_are * early_are - later_aim * early_aim,
        later_are * early_aim + later_aim * early_are,
        later_are * early_bre - later_aim * early_bim + later_bre,
        later_are * early_bim + later_aim * early_bre + later_bim,
    )


def on_device(
    inputs, step_size, decay_rate, frequency, input_proj, output_proj, skip_gain, cotangent
):
    batch_count, row_count, model_width = inputs.shape
    state_count = decay_rate.shape[0]
    damping = jnp.exp(-step_size[:, :, None] * decay_rate)
    phase_turn = step_size[:, :, None] * frequency
    lam_re = damping * jnp.cos(phase_turn)
    lam_im = damping * jnp.sin(phase_turn)
    norm_gain = jnp.sqrt(-jnp.expm1(-2.0 * decay_rate))
    pair_gain = jnp.concatenate([norm_gain, norm_gain])
    flat_in = inputs.reshape(batch_count * row_count, model_width)
    flat_cot = cotangent.reshape(batch_count * row_count, model_width)
    drive_term = (
        jnp.dot(flat_in, input_proj, preferred_element_type=jnp.float32).reshape(
            batch_count, row_count, 2 * state_count
        )
        * pair_gain
    )
    local_fwd = lax.associative_scan(
        complex_combine,
        (lam_re, lam_im, drive_term[..., :state_count], drive_term[..., state_count:]),
        axis=1,
    )
    fwd_summary = (
        local_fwd[0][:, -1],
        local_fwd[1][:, -1],
        local_fwd[2][:, -1],
        local_fwd[3][:, -1],
    )
    adjoint_drive = jnp.dot(flat_cot, output_proj, preferred_element_type=jnp.float32).reshape(
        batch_count, row_count, 2 * state_count
    )
    next_re = jnp.concatenate([lam_re[:, 1:], jnp.ones_like(lam_re[:, :1])], axis=1)
    next_im = jnp.concatenate([-lam_im[:, 1:], jnp.zeros_like(lam_im[:, :1])], axis=1)
    local_back = lax.associative_scan(
        complex_combine,
        (next_re, next_im, adjoint_drive[..., :state_count], adjoint_drive[..., state_count:]),
        axis=1,
        reverse=True,
    )
    first_re = lam_re[:, 0]
    first_im = -lam_im[:, 0]
    back_summary = (
        first_re * local_back[0][:, 0] - first_im * local_back[1][:, 0],
        first_re * local_back[1][:, 0] + first_im * local_back[0][:, 0],
        first_re * local_back[2][:, 0] - first_im * local_back[3][:, 0],
        first_re * local_back[3][:, 0] + first_im * local_back[2][:, 0],
    )
    unit_pair = (
        jnp.ones_like(fwd_summary[0]),
        jnp.zeros_like(fwd_summary[0]),
        jnp.zeros_like(fwd_summary[0]),
        jnp.zeros_like(fwd_summary[0]),
    )
    fwd_carry = prefix(fwd_summary, "context", complex_combine, unit_pair, False)
    back_carry = prefix(back_summary, "context", complex_combine, unit_pair, True)
    carry_re, carry_im = (fwd_carry[2], fwd_carry[3])
    inflow_re, inflow_im = (back_carry[2], back_carry[3])
    state_re = local_fwd[2] + local_fwd[0] * carry_re[:, None] - local_fwd[1] * carry_im[:, None]
    state_im = local_fwd[3] + local_fwd[0] * carry_im[:, None] + local_fwd[1] * carry_re[:, None]
    back_re = (
        local_back[2] + local_back[0] * inflow_re[:, None] - local_back[1] * inflow_im[:, None]
    )
    back_im = (
        local_back[3] + local_back[0] * inflow_im[:, None] + local_back[1] * inflow_re[:, None]
    )
    last_contract = (((1,), (1,)), ((), ()))
    state_pairs = (
        jnp.concatenate([state_re, state_im], axis=-1)
        .astype(jnp.bfloat16)
        .reshape(batch_count * row_count, 2 * state_count)
    )
    mixed = lax.dot_general(
        state_pairs, output_proj, last_contract, preferred_element_type=jnp.float32
    ).reshape(batch_count, row_count, model_width)
    outputs = (mixed + skip_gain * inputs.astype(jnp.float32)).astype(jnp.bfloat16)
    adjoint_pairs = (
        (jnp.concatenate([back_re, back_im], axis=-1) * pair_gain)
        .astype(jnp.bfloat16)
        .reshape(batch_count * row_count, 2 * state_count)
    )
    back_in = lax.dot_general(
        adjoint_pairs, input_proj, last_contract, preferred_element_type=jnp.float32
    ).reshape(batch_count, row_count, model_width)
    input_grad = (back_in + skip_gain * cotangent.astype(jnp.float32)).astype(jnp.bfloat16)
    context_count = lax.axis_size("context")
    grad_scale = float(batch_count * row_count * lax.axis_size("dp") * context_count) ** (-0.5)
    token_contract = (((0,), (0,)), ((), ()))
    grad_in_part = lax.dot_general(
        flat_in, adjoint_pairs, token_contract, preferred_element_type=jnp.float32
    )
    grad_out_part = lax.dot_general(
        flat_cot, state_pairs, token_contract, preferred_element_type=jnp.float32
    )
    shares = lax.psum_scatter(
        jnp.concatenate([grad_in_part, grad_out_part], axis=1) * grad_scale,
        "context",
        scatter_dimension=0,
        tiled=True,
    )
    my_rows = lax.psum(shares, "dp")
    return (outputs, input_grad, my_rows[:, : 2 * state_count], my_rows[:, 2 * state_count :])


def solution(mesh):
    in_specs = (
        P("dp", "context", None),
        P("dp", "context"),
        P(),
        P(),
        P(),
        P(),
        P(),
        P("dp", "context", None),
    )
    out_specs = (
        P("dp", "context", None),
        P("dp", "context", None),
        P("context", None),
        P("context", None),
    )
    return jax.shard_map(
        on_device, mesh=mesh, in_specs=in_specs, out_specs=out_specs, check_vma=False
    )
```

profile of v0, /device:TPU:8, one launch (start us, length us, event | category | flops | bytes accessed | tf_op | source)
XLA Modules:
  0.0 1172.5 jit_solution(17357458822823251579)
XLA Ops:
  8.0 2.7 fusion.12
  29.8 2.9 slice.1317
  32.8 2.9 slice.1323
  37.0 3.0 slice.1333
  40.0 3.0 slice.1320
  43.0 3.0 slice.1326
  46.0 3.0 slice.1328
  223.5 3.0 slice.1453
  226.6 3.0 slice.1458
  229.6 3.0 slice.1496
  253.1 2.6 pad.548
  443.0 4.7 rev.19
  447.8 45.9 %all_gather.32 = f32[32,1,256]{2,1,0:T(1,128)S(1)} all-gather(f32[1,1,256]{2,1,0:T(1,128)} %get-tuple-element.448), channel_id=1, replica_groups=mesh['dp'=8,'context'=32] {'context'}, dimensions={0}, use_global_device_ids=true | all-gather | bytes 33792 | tf_op jit(solution)/shard_map/all_gather | solution.py:9
  493.7 40.8 %all_gather.33 = f32[32,1,256]{2,1,0:T(1,128)S(1)} all-gather(f32[1,1,256]{2,1,0:T(1,128)} %get-tuple-element.447), channel_id=1, replica_groups=mesh['dp'=8,'context'=32] {'context'}, dimensions={0}, use_global_device_ids=true | all-gather | bytes 33792 | tf_op jit(solution)/shard_map/all_gather | solution.py:9
  534.5 41.9 %all_gather.34 = f32[32,1,256]{2,1,0:T(1,128)S(1)} all-gather(f32[1,1,256]{2,1,0:T(1,128)} %get-tuple-element.446), channel_id=1, replica_groups=mesh['dp'=8,'context'=32] {'context'}, dimensions={0}, use_global_device_ids=true | all-gather | bytes 33792 | tf_op jit(solution)/shard_map/all_gather | solution.py:9
  576.4 40.8 %all_gather.35 = f32[32,1,256]{2,1,0:T(1,128)S(1)} all-gather(f32[1,1,256]{2,1,0:T(1,128)} %get-tuple-element.445), channel_id=1, replica_groups=mesh['dp'=8,'context'=32] {'context'}, dimensions={0}, use_global_device_ids=true | all-gather | bytes 33792 | tf_op jit(solution)/shard_map/all_gather | solution.py:9
  617.2 37.7 %while.35 = (s32[]{:T(128)}, f32[1,256]{1,0:T(1,128)}, f32[1,256]{1,0:T(1,128)}, s32[]{:T(128)}, f32[32,1,256]{2,1,0:T(1,128)S(1)}, /*index=5*/f32[32,1,256]{2,1...) while((s32[]{:T(128)}, f32[1,256]{1,0:T(1,128)}, ...), condition=%wide.region_3.4_spmd.clone, body=%wide.region_2.3_spmd.clone.sunk | while | flops 3080 | bytes 8379 | solution.py:20
  654.9 2.6 rev.17
  657.5 2.6 rev.16
  677.2 41.9 %all_gather.31 = f32[32,1,256]{2,1,0:T(1,128)S(1)} all-gather(f32[1,1,256]{2,1,0:T(1,128)S(1)} %slice_add_fusion.64), channel_id=1, replica_groups=mesh['dp'=8,'context'=32] {'context'}, dimensions={0}, use_global_device_ids=true | all-gather | bytes 33792 | tf_op jit(solution)/shard_map/all_gather | solution.py:9
  721.3 40.7 %all_gather.29 = f32[32,1,256]{2,1,0:T(1,128)S(1)} all-gather(f32[1,1,256]{2,1,0:T(1,128)S(1)} %slice_add_fusion.66), channel_id=1, replica_groups=mesh['dp'=8,'context'=32] {'context'}, dimensions={0}, use_global_device_ids=true | all-gather | bytes 33792 | tf_op jit(solution)/shard_map/all_gather | solution.py:9
  763.6 2.6 pad.510
  766.3 2.7 pad.511
  769.7 41.9 %all_gather.28 = f32[32,1,256]{2,1,0:T(1,128)S(1)} all-gather(f32[1,1,256]{2,1,0:T(1,128)S(1)} %slice_add_fusion.67), channel_id=1, replica_groups=mesh['dp'=8,'context'=32] {'context'}, dimensions={0}, use_global_device_ids=true | all-gather | bytes 33792 | tf_op jit(solution)/shard_map/all_gather | solution.py:9
  811.6 2.6 pad.477
  818.2 40.7 %all_gather.30 = f32[32,1,256]{2,1,0:T(1,128)S(1)} all-gather(f32[1,1,256]{2,1,0:T(1,128)S(1)} %slice_add_fusion.65), channel_id=1, replica_groups=mesh['dp'=8,'context'=32] {'context'}, dimensions={0}, use_global_device_ids=true | all-gather | bytes 33792 | tf_op jit(solution)/shard_map/all_gather | solution.py:9
  865.9 2.6 maximum_multiply_fusion
  868.6 5.4 copy.16
  875.1 2.9 fusion.4
  878.1 217.4 %reduce-scatter.4.cloned.1.call-done = f32[32,1024]{1,0:T(8,128)} async-done(((f32[1024,1024]{1,0:T(8,128)}), f32[32,1024]{1,0:T(8,128)}) %reduce-scatter.4.cloned.1.call-update) | async-done | bytes 131088
  1097.5 3.3 fusion.5
  1100.7 62.4 %all-reduce.150.cloned.1.call-done = f32[32,1024]{0,1:T(8,128)} async-done(((f32[32,1024]{0,1:T(8,128)}), f32[32,1024]{0,1:T(8,128)}) %all-reduce.150.cloned.1.call-update) | async-done | bytes 131088 | tf_op jit(solution)/shard_map/psum | solution.py:135
  (908 shorter events, 477.5 us)
Async XLA Ops:
  7.2 272.5 %copy-start = (bf16[1024,512]{1,0:T(8,128)(2,1)S(1)}, bf16[1024,512]{1,0:T(8,128)(2,1)}, u32[]{:S(2)}) copy-start(bf16[1024,512]{1,0:T(8,128)(2,1)} %param.16) | copy-start | bytes 3145732
  7.2 1088.3 %reduce-scatter.4.cloned.1.call-start = ((), (), s32[]{:S(2)}) async-start(), calls=%async_computation.2 | async-start | bytes 4325376
  65.9 103.9 %copy-start.35 = (f32[1,128,256]{2,1,0:T(8,128)}, f32[1,128,256]{2,1,0:T(8,128)S(1)}, u32[]{:S(2)}) copy-start(f32[1,128,256]{2,1,0:T(8,128)S(1)} %get-tuple-element.512) | copy-start | bytes 393220
  290.7 125.0 %copy-start.19 = (f32[1,256,256]{2,1,0:T(8,128)}, f32[1,256,256]{2,1,0:T(8,128)S(1)}, u32[]{:S(2)}) copy-start(f32[1,256,256]{2,1,0:T(8,128)S(1)} %get-tuple-element.471) | copy-start | bytes 786436
  304.0 104.0 %copy-start.36 = (f32[1,128,256]{2,1,0:T(8,128)}, f32[1,128,256]{2,1,0:T(8,128)S(1)}, u32[]{:S(2)}) copy-start(f32[1,128,256]{2,1,0:T(8,128)S(1)} %get-tuple-element.520) | copy-start | bytes 393220
  423.9 233.6 %copy-start.12 = (f32[1,512,256]{2,1,0:T(8,128)S(1)}, f32[1,512,256]{2,1,0:T(8,128)}, u32[]{:S(2)}) copy-start(f32[1,512,256]{2,1,0:T(8,128)} %add.1249) | copy-start | bytes 1572868
  425.4 229.5 %copy-start.13 = (f32[1,512,256]{2,1,0:T(8,128)S(1)}, f32[1,512,256]{2,1,0:T(8,128)}, u32[]{:S(2)}) copy-start(f32[1,512,256]{2,1,0:T(8,128)} %add.1274) | copy-start | bytes 1572868
  426.8 233.4 %copy-start.14 = (f32[1,512,256]{2,1,0:T(8,128)S(1)}, f32[1,512,256]{2,1,0:T(8,128)}, u32[]{:S(2)}) copy-start(f32[1,512,256]{2,1,0:T(8,128)} %add.1276) | copy-start | bytes 1572868
  442.9 219.8 %copy-start.128 = (f32[1,1,256]{2,1,0:T(1,128)S(1)}, f32[1,1,256]{2,1,0:T(1,128)}, u32[]{:S(2)}) copy-start(f32[1,1,256]{2,1,0:T(1,128)} %get-tuple-element.607) | copy-start | bytes 3076
  442.9 219.8 %copy-start.129 = (f32[1,1,256]{2,1,0:T(1,128)S(1)}, f32[1,1,256]{2,1,0:T(1,128)}, u32[]{:S(2)}) copy-start(f32[1,1,256]{2,1,0:T(1,128)} %get-tuple-element.608) | copy-start | bytes 3076
  442.9 219.8 %copy-start.130 = (f32[1,1,256]{2,1,0:T(1,128)S(1)}, f32[1,1,256]{2,1,0:T(1,128)}, u32[]{:S(2)}) copy-start(f32[1,1,256]{2,1,0:T(1,128)} %get-tuple-element.627) | copy-start | bytes 3076
  442.9 219.8 %copy-start.131 = (f32[1,1,256]{2,1,0:T(1,128)S(1)}, f32[1,1,256]{2,1,0:T(1,128)}, u32[]{:S(2)}) copy-start(f32[1,1,256]{2,1,0:T(1,128)} %get-tuple-element.638) | copy-start | bytes 3076
  443.0 219.9 %copy-start.90 = (f32[1,2,256]{2,1,0:T(2,128)S(1)}, f32[1,2,256]{2,1,0:T(2,128)}, u32[]{:S(2)}) copy-start(f32[1,2,256]{2,1,0:T(2,128)} %get-tuple-element.648) | copy-start | bytes 6148
  443.0 219.9 %copy-start.89 = (f32[1,2,256]{2,1,0:T(2,128)S(1)}, f32[1,2,256]{2,1,0:T(2,128)}, u32[]{:S(2)}) copy-start(f32[1,2,256]{2,1,0:T(2,128)} %get-tuple-element.647) | copy-start | bytes 6148
  447.7 215.2 %copy-start.126 = (f32[1,1,256]{2,1,0:T(1,128)S(1)}, f32[1,1,256]{2,1,0:T(1,128)}, u32[]{:S(2)}) copy-start(f32[1,1,256]{2,1,0:T(1,128)} %get-tuple-element.636) | copy-start | bytes 3076
  447.7 215.2 %copy-start.127 = (f32[1,1,256]{2,1,0:T(1,128)S(1)}, f32[1,1,256]{2,1,0:T(1,128)}, u32[]{:S(2)}) copy-start(f32[1,1,256]{2,1,0:T(1,128)} %get-tuple-element.637) | copy-start | bytes 3076
  447.7 215.3 %copy-start.73 = (f32[1,3,256]{2,1,0:T(4,128)S(1)}, f32[1,3,256]{2,1,0:T(4,128)}, u32[]{:S(2)}) copy-start(f32[1,3,256]{2,1,0:T(4,128)} %slice.1200) | copy-start | bytes 9220
  447.7 215.3 %copy-start.74 = (f32[1,3,256]{2,1,0:T(4,128)S(1)}, f32[1,3,256]{2,1,0:T(4,128)}, u32[]{:S(2)}) copy-start(f32[1,3,256]{2,1,0:T(4,128)} %slice.1231) | copy-start | bytes 9220
  447.7 215.3 %copy-start.81 = (f32[1,3,256]{2,1,0:T(4,128)S(1)}, f32[1,3,256]{2,1,0:T(4,128)}, u32[]{:S(2)}) copy-start(f32[1,3,256]{2,1,0:T(4,128)} %slice.1235) | copy-start | bytes 9220
  447.7 215.3 %copy-start.82 = (f32[1,3,256]{2,1,0:T(4,128)S(1)}, f32[1,3,256]{2,1,0:T(4,128)}, u32[]{:S(2)}) copy-start(f32[1,3,256]{2,1,0:T(4,128)} %slice.1239) | copy-start | bytes 9220
  447.7 215.4 %copy-start.122 = (f32[1,1,256]{2,1,0:T(1,128)S(1)}, f32[1,1,256]{2,1,0:T(1,128)}, u32[]{:S(2)}) copy-start(f32[1,1,256]{2,1,0:T(1,128)} %slice.1531) | copy-start | bytes 3076
  447.7 215.4 %copy-start.120 = (f32[1,1,256]{2,1,0:T(1,128)S(1)}, f32[1,1,256]{2,1,0:T(1,128)}, u32[]{:S(2)}) copy-start(f32[1,1,256]{2,1,0:T(1,128)} %slice.1508) | copy-start | bytes 3076
  447.8 215.6 %copy-start.63 = (f32[1,7,256]{2,1,0:T(8,128)S(1)}, f32[1,7,256]{2,1,0:T(8,128)}, u32[]{:S(2)}) copy-start(f32[1,7,256]{2,1,0:T(8,128)} %slice.1190) | copy-start | bytes 21508
  447.8 215.6 %copy-start.64 = (f32[1,7,256]{2,1,0:T(8,128)S(1)}, f32[1,7,256]{2,1,0:T(8,128)}, u32[]{:S(2)}) copy-start(f32[1,7,256]{2,1,0:T(8,128)} %slice.1237) | copy-start | bytes 21508
  447.8 215.6 %copy-start.77 = (f32[1,7,256]{2,1,0:T(8,128)S(1)}, f32[1,7,256]{2,1,0:T(8,128)}, u32[]{:S(2)}) copy-start(f32[1,7,256]{2,1,0:T(8,128)} %slice.1241) | copy-start | bytes 21508
  447.8 215.6 %copy-start.78 = (f32[1,7,256]{2,1,0:T(8,128)S(1)}, f32[1,7,256]{2,1,0:T(8,128)}, u32[]{:S(2)}) copy-start(f32[1,7,256]{2,1,0:T(8,128)} %slice.1245) | copy-start | bytes 21508
  493.7 169.8 %copy-start.119 = (f32[1,1,256]{2,1,0:T(1,128)S(1)}, f32[1,1,256]{2,1,0:T(1,128)}, u32[]{:S(2)}) copy-start(f32[1,1,256]{2,1,0:T(1,128)} %slice.1536) | copy-start | bytes 3076
  762.0 97.0 %copy-start.75 = (f32[1,256]{1,0:T(1,128)S(1)}, f32[1,256]{1,0:T(1,128)}, u32[]{:S(2)}) copy-start(f32[1,256]{1,0:T(1,128)} %custom-call) | copy-start | bytes 3076
  762.0 97.0 %copy-start.76 = (f32[1,256]{1,0:T(1,128)S(1)}, f32[1,256]{1,0:T(1,128)}, u32[]{:S(2)}) copy-start(f32[1,256]{1,0:T(1,128)} %custom-call.1) | copy-start | bytes 3076
  763.6 96.7 %copy-start.72 = (f32[1,256]{1,0:T(1,128)S(1)}, f32[1,256]{1,0:T(1,128)}, u32[]{:S(2)}) copy-start(f32[1,256]{1,0:T(1,128)} %get-tuple-element.346) | copy-start | bytes 3076
  874.0 223.5 %copy-start.25 = (bf16[512,256]{1,0:T(8,128)(2,1)S(1)}, bf16[512,256]{1,0:T(8,128)(2,1)}, u32[]{:S(2)}) copy-start(bf16[512,256]{1,0:T(8,128)(2,1)} %copy-done.24) | copy-start | bytes 786436
  874.0 289.1 %all-reduce.150.cloned.1.call-start = ((), (), s32[]{:S(2)}) async-start(), calls=%async_computation.1 | async-start | bytes 1048576 | tf_op jit(solution)/shard_map/psum | solution.py:135
  (104 other events, 1177.9 us)
Sparse Core Ops, SparseCore 0:
  874.1 221.3 reduce-scatter.3
  1097.8 65.2 all-reduce.149
where the time goes:
time: 1190 us; the launch traced here: 1170 us
  local copies, waits for them, and re-layouts  405 us (34%)
  blocking collectives  335 us (28%)
  waiting for transfers between devices  280 us (24%)
  other arithmetic  124 us (10%)
  between operations  17 us (1%)
    all_gather x8, blocking collectives, prefix(): everything = jax.tree.map(lambda part: lax.all_gather(part, axis), x)  335 us
    unnamed x3, waiting for transfers between devices  217 us
    slice x132, local copies, waits for them, and re-layouts, on_device(): lax.associative_scan(complex_combine, (next_re, next_im, adjoint_drive[.....  185 us
    slice x120, local copies, waits for them, and re-layouts, on_device(): lax.associative_scan(complex_combine, (lam_re, lam_im, drive_term[..., :s...  148 us
    psum x1, waiting for transfers between devices, on_device(): my_rows = lax.psum(shares, 'dp')  62.4 us
    select_n x64, other arithmetic, lap(): return jax.tree.map(lambda a, b: jnp.where(reached, a, b), new, before)  38.3 us
  transfers between devices with their start and end apart: 2, of which 2 were waited for; matrix products, arithmetic and copies ran while one was open for 1% of the time, Pallas kernels for 0%

commit v1 on v0

--- a/solution.py
+++ b/solution.py
@@ -132,7 +132,7 @@
         scatter_dimension=0,
         tiled=True,
     )
-    my_rows = lax.psum(shares, "dp")
+    my_rows = jnp.sum(lax.all_gather(shares, "dp"), axis=0)
     return (outputs, input_grad, my_rows[:, : 2 * state_count], my_rows[:, 2 * state_count :])
 
 

time: 1190 us -> 1150 us (0.966)
  waiting for transfers between devices: 280 us -> 243 us
    reduce_scatter x0 -> x1, waiting for transfers between devices: none -> 221 us  [on_device(): lax.psum_scatter(jnp.concatenate([grad_in_part, grad_out_part], axis=1) *...]
    unnamed x3 -> x2, waiting for transfers between devices: 217 us -> 0.03 us
    psum x1 -> x0, waiting for transfers between devices: 62.4 us -> none  [on_device(): my_rows = lax.psum(shares, 'dp')]
    all_gather x0 -> x1, waiting for transfers between devices: none -> 21.9 us  [on_device(): my_rows = jnp.sum(lax.all_gather(shares, 'dp'), axis=0)]
  transfers between devices with their start and end apart: 2 -> 2, of which waited for: 2 -> 2; matrix products, arithmetic and copies ran while one was open for 1% -> 0% of each run, Pallas kernels for 0% -> 0%
where the time goes in v1:
time: 1150 us; the launch traced here: 1130 us
  local copies, waits for them, and re-layouts  400 us (35%)
  blocking collectives  335 us (29%)
  waiting for transfers between devices  243 us (21%)
  other arithmetic  127 us (11%)
  between operations  17.1 us (1%)
    all_gather x8, blocking collectives, prefix(): everything = jax.tree.map(lambda part: lax.all_gather(part, axis), x)  335 us
    reduce_scatter x1, waiting for transfers between devices, on_device(): lax.psum_scatter(jnp.concatenate([grad_in_part, grad_out_part], axis=1) *...  221 us
    slice x132, local copies, waits for them, and re-layouts, on_device(): lax.associative_scan(complex_combine, (next_re, next_im, adjoint_drive[.....  185 us
    slice x120, local copies, waits for them, and re-layouts, on_device(): lax.associative_scan(complex_combine, (lam_re, lam_im, drive_term[..., :s...  148 us
    select_n x64, other arithmetic, lap(): return jax.tree.map(lambda a, b: jnp.where(reached, a, b), new, before)  40.6 us
    add x28, other arithmetic, complex_combine(): later_are * early_bim + later_aim * early_bre + later_bim  23.6 us
    pad x64, local copies, waits for them, and re-layouts, on_device(): lax.associative_scan(complex_combine, (next_re, next_im, adjoint_drive[.....  23.1 us
  transfers between devices with their start and end apart: 2, of which 2 were waited for; matrix products, arithmetic and copies ran while one was open for 0% of the time, Pallas kernels for 0%

profile of v1, /device:TPU:8, one launch (start us, length us, event | category | flops | bytes accessed | tf_op | source)
XLA Modules:
  0.0 1133.1 jit_solution(5485342215908645795)
XLA Ops:
  8.0 2.7 fusion.12
  29.5 3.0 slice.1317
  32.4 3.0 slice.1323
  36.7 3.0 slice.1333
  39.7 3.0 slice.1320
  42.7 3.0 slice.1326
  45.7 3.0 slice.1328
  223.1 3.0 slice.1453
  226.1 3.0 slice.1458
  229.1 3.0 slice.1496
  442.6 4.7 rev.19
  447.4 45.9 %all_gather.38 = f32[32,1,256]{2,1,0:T(1,128)S(1)} all-gather(f32[1,1,256]{2,1,0:T(1,128)} %get-tuple-element.440), channel_id=1, replica_groups=mesh['dp'=8,'context'=32] {'context'}, dimensions={0}, use_global_device_ids=true | all-gather | bytes 33792 | tf_op jit(solution)/shard_map/all_gather | solution.py:9
  493.3 40.8 %all_gather.39 = f32[32,1,256]{2,1,0:T(1,128)S(1)} all-gather(f32[1,1,256]{2,1,0:T(1,128)} %get-tuple-element.439), channel_id=1, replica_groups=mesh['dp'=8,'context'=32] {'context'}, dimensions={0}, use_global_device_ids=true | all-gather | bytes 33792 | tf_op jit(solution)/shard_map/all_gather | solution.py:9
  534.1 41.9 %all_gather.40 = f32[32,1,256]{2,1,0:T(1,128)S(1)} all-gather(f32[1,1,256]{2,1,0:T(1,128)} %get-tuple-element.438), channel_id=1, replica_groups=mesh['dp'=8,'context'=32] {'context'}, dimensions={0}, use_global_device_ids=true | all-gather | bytes 33792 | tf_op jit(solution)/shard_map/all_gather | solution.py:9
  576.0 40.8 %all_gather.41 = f32[32,1,256]{2,1,0:T(1,128)S(1)} all-gather(f32[1,1,256]{2,1,0:T(1,128)} %get-tuple-element.437), channel_id=1, replica_groups=mesh['dp'=8,'context'=32] {'context'}, dimensions={0}, use_global_device_ids=true | all-gather | bytes 33792 | tf_op jit(solution)/shard_map/all_gather | solution.py:9
  616.8 40.0 %while.35 = (s32[]{:T(128)}, f32[1,256]{1,0:T(1,128)}, f32[1,256]{1,0:T(1,128)}, s32[]{:T(128)}, f32[32,1,256]{2,1,0:T(1,128)S(1)}, /*index=5*/f32[32,1,256]{2,1...) while((s32[]{:T(128)}, f32[1,256]{1,0:T(1,128)}, ...), condition=%wide.region_3.4_spmd.clone, body=%wide.region_2.3_spmd.clone.sunk | while | flops 3080 | bytes 8379 | solution.py:20
  656.9 2.6 rev.17
  659.5 2.6 rev.16
  662.2 2.6 rev.18
  679.3 41.9 %all_gather.37 = f32[32,1,256]{2,1,0:T(1,128)S(1)} all-gather(f32[1,1,256]{2,1,0:T(1,128)S(1)} %slice_add_fusion.64), channel_id=1, replica_groups=mesh['dp'=8,'context'=32] {'context'}, dimensions={0}, use_global_device_ids=true | all-gather | bytes 33792 | tf_op jit(solution)/shard_map/all_gather | solution.py:9
  723.3 40.7 %all_gather.35 = f32[32,1,256]{2,1,0:T(1,128)S(1)} all-gather(f32[1,1,256]{2,1,0:T(1,128)S(1)} %slice_add_fusion.66), channel_id=1, replica_groups=mesh['dp'=8,'context'=32] {'context'}, dimensions={0}, use_global_device_ids=true | all-gather | bytes 33792 | tf_op jit(solution)/shard_map/all_gather | solution.py:9
  765.7 2.7 pad.510
  768.4 2.7 pad.511
  771.8 41.9 %all_gather.34 = f32[32,1,256]{2,1,0:T(1,128)S(1)} all-gather(f32[1,1,256]{2,1,0:T(1,128)S(1)} %slice_add_fusion.67), channel_id=1, replica_groups=mesh['dp'=8,'context'=32] {'context'}, dimensions={0}, use_global_device_ids=true | all-gather | bytes 33792 | tf_op jit(solution)/shard_map/all_gather | solution.py:9
  813.7 2.6 pad.477
  817.0 2.6 pad.476
  820.3 40.7 %all_gather.36 = f32[32,1,256]{2,1,0:T(1,128)S(1)} all-gather(f32[1,1,256]{2,1,0:T(1,128)S(1)} %slice_add_fusion.65), channel_id=1, replica_groups=mesh['dp'=8,'context'=32] {'context'}, dimensions={0}, use_global_device_ids=true | all-gather | bytes 33792 | tf_op jit(solution)/shard_map/all_gather | solution.py:9
  868.0 2.6 maximum_multiply_fusion
  870.7 5.4 copy.14
  876.1 221.4 %reduce-scatter.4.cloned.1.call-done = f32[32,1024]{1,0:T(8,128)} async-done(((f32[1024,1024]{1,0:T(8,128)}), f32[32,1024]{1,0:T(8,128)}) %reduce-scatter.4.cloned.1.call-update) | async-done | bytes 131088 | tf_op jit(solution)/shard_map/reduce_scatter | solution.py:129
  1097.6 3.1 fusion.5
  1102.4 21.9 %all-gather.3.cloned.1.call-done = f32[256,1024]{1,0:T(8,128)} async-done(((f32[32,1024]{1,0:T(8,128)}), f32[256,1024]{1,0:T(8,128)}) %all-gather.3.cloned.1.call-update) | async-done | bytes 1048592 | tf_op jit(solution)/shard_map/all_gather | solution.py:135
  (910 shorter events, 475.0 us)
Async XLA Ops:
  7.2 1090.3 %reduce-scatter.4.cloned.1.call-start = ((), (), s32[]{:S(2)}) async-start(), calls=%async_computation.2 | async-start | bytes 4325376 | tf_op jit(solution)/shard_map/reduce_scatter | solution.py:129
  65.6 103.9 %copy-start.36 = (f32[1,128,256]{2,1,0:T(8,128)}, f32[1,128,256]{2,1,0:T(8,128)S(1)}, u32[]{:S(2)}) copy-start(f32[1,128,256]{2,1,0:T(8,128)S(1)} %get-tuple-element.502) | copy-start | bytes 393220
  290.4 125.1 %copy-start.19 = (f32[1,256,256]{2,1,0:T(8,128)}, f32[1,256,256]{2,1,0:T(8,128)S(1)}, u32[]{:S(2)}) copy-start(f32[1,256,256]{2,1,0:T(8,128)S(1)} %get-tuple-element.463) | copy-start | bytes 786436
  303.7 104.0 %copy-start.37 = (f32[1,128,256]{2,1,0:T(8,128)}, f32[1,128,256]{2,1,0:T(8,128)S(1)}, u32[]{:S(2)}) copy-start(f32[1,128,256]{2,1,0:T(8,128)S(1)} %get-tuple-element.510) | copy-start | bytes 393220
  423.7 235.8 %copy-start.12 = (f32[1,512,256]{2,1,0:T(8,128)S(1)}, f32[1,512,256]{2,1,0:T(8,128)}, u32[]{:S(2)}) copy-start(f32[1,512,256]{2,1,0:T(8,128)} %add.1247) | copy-start | bytes 1572868
  425.1 231.7 %copy-start.13 = (f32[1,512,256]{2,1,0:T(8,128)S(1)}, f32[1,512,256]{2,1,0:T(8,128)}, u32[]{:S(2)}) copy-start(f32[1,512,256]{2,1,0:T(8,128)} %add.1272) | copy-start | bytes 1572868
  426.5 235.7 %copy-start.14 = (f32[1,512,256]{2,1,0:T(8,128)S(1)}, f32[1,512,256]{2,1,0:T(8,128)}, u32[]{:S(2)}) copy-start(f32[1,512,256]{2,1,0:T(8,128)} %add.1274) | copy-start | bytes 1572868
  442.5 222.3 %copy-start.129 = (f32[1,1,256]{2,1,0:T(1,128)S(1)}, f32[1,1,256]{2,1,0:T(1,128)}, u32[]{:S(2)}) copy-start(f32[1,1,256]{2,1,0:T(1,128)} %get-tuple-element.599) | copy-start | bytes 3076
  442.5 222.3 %copy-start.130 = (f32[1,1,256]{2,1,0:T(1,128)S(1)}, f32[1,1,256]{2,1,0:T(1,128)}, u32[]{:S(2)}) copy-start(f32[1,1,256]{2,1,0:T(1,128)} %get-tuple-element.600) | copy-start | bytes 3076
  442.5 222.3 %copy-start.131 = (f32[1,1,256]{2,1,0:T(1,128)S(1)}, f32[1,1,256]{2,1,0:T(1,128)}, u32[]{:S(2)}) copy-start(f32[1,1,256]{2,1,0:T(1,128)} %get-tuple-element.619) | copy-start | bytes 3076
  442.5 222.3 %copy-start.132 = (f32[1,1,256]{2,1,0:T(1,128)S(1)}, f32[1,1,256]{2,1,0:T(1,128)}, u32[]{:S(2)}) copy-start(f32[1,1,256]{2,1,0:T(1,128)} %get-tuple-element.630) | copy-start | bytes 3076
  442.5 222.3 %copy-start.91 = (f32[1,2,256]{2,1,0:T(2,128)S(1)}, f32[1,2,256]{2,1,0:T(2,128)}, u32[]{:S(2)}) copy-start(f32[1,2,256]{2,1,0:T(2,128)} %get-tuple-element.640) | copy-start | bytes 6148
  442.6 222.3 %copy-start.90 = (f32[1,2,256]{2,1,0:T(2,128)S(1)}, f32[1,2,256]{2,1,0:T(2,128)}, u32[]{:S(2)}) copy-start(f32[1,2,256]{2,1,0:T(2,128)} %get-tuple-element.639) | copy-start | bytes 6148
  447.3 217.6 %copy-start.127 = (f32[1,1,256]{2,1,0:T(1,128)S(1)}, f32[1,1,256]{2,1,0:T(1,128)}, u32[]{:S(2)}) copy-start(f32[1,1,256]{2,1,0:T(1,128)} %get-tuple-element.628) | copy-start | bytes 3076
  447.3 217.6 %copy-start.128 = (f32[1,1,256]{2,1,0:T(1,128)S(1)}, f32[1,1,256]{2,1,0:T(1,128)}, u32[]{:S(2)}) copy-start(f32[1,1,256]{2,1,0:T(1,128)} %get-tuple-element.629) | copy-start | bytes 3076
  447.3 217.7 %copy-start.74 = (f32[1,3,256]{2,1,0:T(4,128)S(1)}, f32[1,3,256]{2,1,0:T(4,128)}, u32[]{:S(2)}) copy-start(f32[1,3,256]{2,1,0:T(4,128)} %slice.1200) | copy-start | bytes 9220
  447.3 217.7 %copy-start.75 = (f32[1,3,256]{2,1,0:T(4,128)S(1)}, f32[1,3,256]{2,1,0:T(4,128)}, u32[]{:S(2)}) copy-start(f32[1,3,256]{2,1,0:T(4,128)} %slice.1231) | copy-start | bytes 9220
  447.3 217.8 %copy-start.82 = (f32[1,3,256]{2,1,0:T(4,128)S(1)}, f32[1,3,256]{2,1,0:T(4,128)}, u32[]{:S(2)}) copy-start(f32[1,3,256]{2,1,0:T(4,128)} %slice.1235) | copy-start | bytes 9220
  447.3 217.8 %copy-start.83 = (f32[1,3,256]{2,1,0:T(4,128)S(1)}, f32[1,3,256]{2,1,0:T(4,128)}, u32[]{:S(2)}) copy-start(f32[1,3,256]{2,1,0:T(4,128)} %slice.1239) | copy-start | bytes 9220
  447.3 217.8 %copy-start.123 = (f32[1,1,256]{2,1,0:T(1,128)S(1)}, f32[1,1,256]{2,1,0:T(1,128)}, u32[]{:S(2)}) copy-start(f32[1,1,256]{2,1,0:T(1,128)} %slice.1531) | copy-start | bytes 3076
  447.3 217.8 %copy-start.121 = (f32[1,1,256]{2,1,0:T(1,128)S(1)}, f32[1,1,256]{2,1,0:T(1,128)}, u32[]{:S(2)}) copy-start(f32[1,1,256]{2,1,0:T(1,128)} %slice.1508) | copy-start | bytes 3076
  447.3 218.0 %copy-start.64 = (f32[1,7,256]{2,1,0:T(8,128)S(1)}, f32[1,7,256]{2,1,0:T(8,128)}, u32[]{:S(2)}) copy-start(f32[1,7,256]{2,1,0:T(8,128)} %slice.1190) | copy-start | bytes 21508
  447.4 218.0 %copy-start.65 = (f32[1,7,256]{2,1,0:T(8,128)S(1)}, f32[1,7,256]{2,1,0:T(8,128)}, u32[]{:S(2)}) copy-start(f32[1,7,256]{2,1,0:T(8,128)} %slice.1237) | copy-start | bytes 21508
  447.4 218.0 %copy-start.78 = (f32[1,7,256]{2,1,0:T(8,128)S(1)}, f32[1,7,256]{2,1,0:T(8,128)}, u32[]{:S(2)}) copy-start(f32[1,7,256]{2,1,0:T(8,128)} %slice.1241) | copy-start | bytes 21508
  447.4 218.0 %copy-start.79 = (f32[1,7,256]{2,1,0:T(8,128)S(1)}, f32[1,7,256]{2,1,0:T(8,128)}, u32[]{:S(2)}) copy-start(f32[1,7,256]{2,1,0:T(8,128)} %slice.1245) | copy-start | bytes 21508
  493.3 172.2 %copy-start.120 = (f32[1,1,256]{2,1,0:T(1,128)S(1)}, f32[1,1,256]{2,1,0:T(1,128)}, u32[]{:S(2)}) copy-start(f32[1,1,256]{2,1,0:T(1,128)} %slice.1536) | copy-start | bytes 3076
  764.0 97.0 %copy-start.76 = (f32[1,256]{1,0:T(1,128)S(1)}, f32[1,256]{1,0:T(1,128)}, u32[]{:S(2)}) copy-start(f32[1,256]{1,0:T(1,128)} %custom-call) | copy-start | bytes 3076
  764.0 97.0 %copy-start.77 = (f32[1,256]{1,0:T(1,128)S(1)}, f32[1,256]{1,0:T(1,128)}, u32[]{:S(2)}) copy-start(f32[1,256]{1,0:T(1,128)} %custom-call.1) | copy-start | bytes 3076
  765.7 96.7 %copy-start.73 = (f32[1,256]{1,0:T(1,128)S(1)}, f32[1,256]{1,0:T(1,128)}, u32[]{:S(2)}) copy-start(f32[1,256]{1,0:T(1,128)} %get-tuple-element.346) | copy-start | bytes 3076
  876.0 221.5 %copy-start.25 = (bf16[512,256]{1,0:T(8,128)(2,1)S(1)}, bf16[512,256]{1,0:T(8,128)(2,1)}, u32[]{:S(2)}) copy-start(bf16[512,256]{1,0:T(8,128)(2,1)} %copy-done.24) | copy-start | bytes 786436
  876.0 221.5 %copy-start.135 = (f32[1024]{0:T(1024)S(1)}, f32[1024]{0:T(1024)}, u32[]{:S(2)}) copy-start(f32[1024]{0:T(1024)} %param.18) | copy-start | bytes 12292
  876.1 248.2 %all-gather.3.cloned.1.call-start = ((), (), s32[]{:S(2)}) async-start(), calls=%async_computation.1 | async-start | bytes 1179648 | tf_op jit(solution)/shard_map/all_gather | solution.py:135
  (106 other events, 1196.9 us)
Sparse Core Ops, SparseCore 0:
  876.2 221.2 reduce-scatter.3
  1099.4 24.8 all-gather.2
